TPU v7x, 32 devices: a whole 2x2x4 slice. The times are simulated.
32 devices in a mesh: groups: 2 (over y), ctx: 4 (over z), tp: 4 (over x, core).
Axes of the slice: x: 2, y: 2, z: 4, core: 2. Of those that a mesh axis runs over, the one named last changes fastest.
Arguments:
- queries: bfloat16 [1152, 8192], P(('groups', 'ctx'), 'tp'), parts along dimension 0, may hold values from -6 to 6
- keys: bfloat16 [1152, 1024], P(('groups', 'ctx'), 'tp'), parts along dimension 0, may hold values from -6 to 6
- values: bfloat16 [1152, 1024], P(('groups', 'ctx'), 'tp'), parts along dimension 0, may hold values from -6 to 6
- residual: bfloat16 [1152, 8192], P(('groups', 'ctx'), 'tp'), parts along dimension 0, may hold values from -4 to 4
- out_weight: bfloat16 [8192, 8192], P('tp', 'ctx'), may hold values from -0.0625 to 0.0625
- value_head: bfloat16 [8192], P('tp'), may hold values from -0.5 to 0.5
- segment_ids: int32 [1152], P(('groups', 'ctx')), parts along dimension 0, may hold values from 0 to 3, as said below
- positions: int32 [1152], P(('groups', 'ctx')), parts along dimension 0, may hold values from 0 to 251, as said below
- turn_ids: int32 [1152], P(('groups', 'ctx')), parts along dimension 0, may hold values from 0 to 15, as said below
Outputs:
- hidden_out: bfloat16 [1152, 8192], P(('groups', 'ctx'), 'tp'), parts along dimension 0
- turn_means: float32 [32], P('groups'), parts along dimension 0
There are 2 independent parts, one for each index of `groups`. A program takes and returns all parts, laid end to end along the dimension named above; an argument that names none is the same for every part. Nothing has to cross between parts.
Inputs may be any that keep to these rules, and one draw needn't show every extreme that they name: `segment_ids`: in token order (the stored order reverted) segment ids never fall; the sequence holds 4 rollouts of 36 to 252 tokens, one of exactly 252. `positions`: A row's position is its token's offset from the first token of its rollout. `turn_ids`: A row's turn id is 4 times its segment id plus how many of its rollout's three turn starts lie at or before its position; turn starts lie at positions 1 to the rollout's length minus 1 and may coincide.
All inputs are finite; a program needn't handle non-finite values.
Results may differ from a plain program's by a relative error of at most 0.013.
Values may be sent and summed in bfloat16 or wider, within the bound.
A program may use at most 64 MiB of HBM per device.

v0:
```python
import math

import jax
import jax.numpy as jnp
from jax import lax
from jax.sharding import PartitionSpec as P

HEAD_SIZE = 128
TURNS = 16


def shards(
    queries, keys, values, residual, out_weight, value_head, segment_ids, positions, turn_ids
):
    tok_rows = queries.shape[0]
    kv_heads = keys.shape[1] // HEAD_SIZE
    query_head_group = queries.shape[1] // keys.shape[1]
    query_rows = query_head_group * tok_rows
    score_scale = 1.0 / math.sqrt(HEAD_SIZE)
    grouped = (
        queries.reshape(tok_rows, kv_heads, query_head_group, HEAD_SIZE)
        .transpose(1, 2, 0, 3)
        .reshape(kv_heads, query_rows, HEAD_SIZE)
    )
    seg_rows = jnp.tile(segment_ids, query_head_group)
    pos_rows = jnp.tile(positions, query_head_group)

    def update(running, key_block, value_block, seg_block, pos_block):
        allowed = (seg_rows[:, None] == seg_block[None, :]) & (
            pos_block[None, :] <= pos_rows[:, None]
        )
        numerator, row_max, denominator = running
        scores = (
            jnp.einsum("hqd,khd->hqk", grouped, key_block, preferred_element_type=jnp.float32)
            * score_scale
        )
        scores = jnp.where(allowed[None], scores, -1e30)
        new_max = jnp.maximum(row_max, jnp.max(scores, axis=2))
        weights = jnp.where(allowed[None], jnp.exp(scores - new_max[..., None]), 0.0)
        factor = jnp.exp(row_max - new_max)
        denominator = denominator * factor + jnp.sum(weights, axis=2)
        product = jnp.einsum(
            "hqk,khd->hqd",
            weights.astype(jnp.bfloat16),
            value_block,
            preferred_element_type=jnp.float32,
        )
        numerator = numerator * factor[..., None] + product
        return (numerator, new_max, denominator)

    initial = (
        jnp.zeros((kv_heads, query_rows, HEAD_SIZE), jnp.float32),
        jnp.full((kv_heads, query_rows), -1e30, jnp.float32),
        jnp.zeros((kv_heads, query_rows), jnp.float32),
    )
    running = initial
    key_piece = lax.all_gather(keys, "ctx", axis=0, tiled=True)
    value_piece = lax.all_gather(values, "ctx", axis=0, tiled=True)
    seg_piece = lax.all_gather(segment_ids, "ctx", axis=0, tiled=True)
    pos_piece = lax.all_gather(positions, "ctx", axis=0, tiled=True)
    row_count = key_piece.shape[0]
    key_piece = key_piece.reshape(row_count, kv_heads, HEAD_SIZE)
    value_piece = value_piece.reshape(row_count, kv_heads, HEAD_SIZE)
    block_width = math.gcd(row_count, 512)
    block_steps = row_count // block_width
    stacked = (
        key_piece.reshape(block_steps, block_width, kv_heads, HEAD_SIZE),
        value_piece.reshape(block_steps, block_width, kv_heads, HEAD_SIZE),
        seg_piece.reshape(block_steps, block_width),
        pos_piece.reshape(block_steps, block_width),
    )

    def block_step(running_state, block_set):
        return (update(running_state, block_set[0], block_set[1], block_set[2], block_set[3]), None)

    running, _ = lax.scan(block_step, running, stacked)
    numerator, row_max, denominator = running
    attention = (numerator / denominator[..., None]).reshape(
        kv_heads, query_head_group, tok_rows, HEAD_SIZE
    )
    attention = (
        attention.transpose(2, 0, 1, 3)
        .reshape(tok_rows, kv_heads * query_head_group * HEAD_SIZE)
        .astype(jnp.bfloat16)
    )
    partial_value = jnp.dot(
        lax.all_gather(attention, "ctx", axis=0, tiled=True),
        out_weight,
        preferred_element_type=jnp.float32,
    ).astype(jnp.bfloat16)
    term_rows = lax.all_to_all(
        partial_value, "ctx", split_axis=0, concat_axis=1, tiled=True
    ).astype(jnp.float32)
    summed = lax.psum_scatter(
        term_rows.astype(jnp.bfloat16), "tp", scatter_dimension=1, tiled=True
    ).astype(jnp.float32)
    hidden_out = (residual.astype(jnp.float32) + summed).astype(jnp.bfloat16)
    token_score = jnp.dot(hidden_out, value_head, preferred_element_type=jnp.float32)
    one_hot = (turn_ids[:, None] == jnp.arange(TURNS, dtype=jnp.int32)[None, :]).astype(jnp.float32)
    local_sum = jnp.dot(token_score, one_hot, precision=lax.Precision.HIGHEST)
    local_count = jnp.where(lax.axis_index("tp") == 0, jnp.sum(one_hot, axis=0), 0.0)
    totals, counts = lax.psum((local_sum, local_count), ("ctx", "tp"))
    turn_means = totals / jnp.maximum(counts, 1.0)
    return (hidden_out, turn_means)


def solution(mesh):
    return jax.shard_map(
        shards,
        mesh=mesh,
        in_specs=(
            P(("groups", "ctx"), "tp"),
            P(("groups", "ctx"), "tp"),
            P(("groups", "ctx"), "tp"),
            P(("groups", "ctx"), "tp"),
            P("tp", "ctx"),
            P("tp"),
            P(("groups", "ctx")),
            P(("groups", "ctx")),
            P(("groups", "ctx")),
        ),
        out_specs=(P(("groups", "ctx"), "tp"), P("groups")),
        check_vma=False,
    )
```

profile of v0, /device:TPU:0, one launch (start us, length us, event | category | flops | bytes accessed | tf_op | source)
XLA Modules:
  0.0 258.4 jit_solution(10053838486972242503)
XLA Ops:
  7.3 1.2 dynamic-slice
  9.2 0.9 dynamic-update-slice
  10.0 0.9 dynamic-update-slice.1
  10.9 10.0 %all-reduce.2 = (s32[576]{0:T(1024)S(1)}, s32[576]{0:T(1024)S(1)}) all-reduce(s32[576]{0:T(1024)S(1)} %dynamic-update-slice, s32[576]{0:T(1024)S(1)} %dynamic-update-slice.1), channel_id=1, replica_groups=mesh['groups'=2,'ctx'=4,'tp'=4] {'ctx'}, use_global_device_ids=true, to_apply=%add | all-reduce | flops 1152 | bytes 9216
  21.1 1.2 copy.26
  22.3 0.2 copy.18
  22.5 14.0 %all_gather.17 = bf16[576,256]{1,0:T(8,128)(2,1)S(1)} all-gather(bf16[144,256]{1,0:T(8,128)(2,1)S(1)} %copy-done.2), channel_id=1, replica_groups=mesh['groups'=2,'ctx'=4,'tp'=4] {'ctx'}, dimensions={0}, use_global_device_ids=true | all-gather | bytes 368640 | tf_op jit(solution)/shard_map/all_gather | solution.py:57
  36.6 14.3 %all_gather.18 = bf16[576,256]{1,0:T(8,128)(2,1)S(1)} all-gather(bf16[144,256]{1,0:T(8,128)(2,1)S(1)} %copy-done.3), channel_id=1, replica_groups=mesh['groups'=2,'ctx'=4,'tp'=4] {'ctx'}, dimensions={0}, use_global_device_ids=true | all-gather | bytes 368640 | tf_op jit(solution)/shard_map/all_gather | solution.py:58
  51.0 16.4 %while.15 = (s32[]{:T(128)}, f32[2,1152,128]{2,1,0:T(8,128)S(1)}, f32[2,1152]{1,0:T(2,128)S(1)}, f32[2,1152]{1,0:T(2,128)S(1)}, s32[9,64]{1,0:T(8,128)S(1)}, /*i...) while((s32[]{:T(128)}, f32[2,1152,128]{2,1,0:T(8,128)S(1)}, ...), condition=%wide.region_3.4_spmd.clone, body=%wide.region_0.3_spmd.clone.sunk | while | flops 77942016 | bytes 5397265 | solution.py:76
  51.4 0.4 fusion.35
  51.8 0.1 fusion.37
  52.0 0.8 convolution_add_fusion.2
  53.2 0.4 fusion.35
  53.6 0.1 fusion.37
  53.8 0.8 convolution_add_fusion.2
  55.0 0.4 fusion.35
  55.4 0.1 fusion.37
  55.6 0.8 convolution_add_fusion.2
  56.9 0.4 fusion.35
  57.2 0.1 fusion.37
  57.4 0.8 convolution_add_fusion.2
  58.7 0.4 fusion.35
  59.1 0.1 fusion.37
  59.2 0.8 convolution_add_fusion.2
  60.5 0.4 fusion.35
  60.9 0.1 fusion.37
  61.1 0.8 convolution_add_fusion.2
  62.3 0.4 fusion.35
  62.7 0.1 fusion.37
  62.9 0.8 convolution_add_fusion.2
  64.1 0.4 fusion.35
  64.5 0.1 fusion.37
  64.7 0.8 convolution_add_fusion.2
  65.9 0.4 fusion.35
  66.5 0.8 convolution_add_fusion.2
  67.3 0.4 divide_convert_fusion
  67.7 0.2 copy.21
  67.9 1.0 copy.35
  68.9 50.1 %all-gather.2.cloned.1.call-done = bf16[576,2048]{1,0:T(8,128)(2,1)} async-done(((bf16[144,2048]{1,0:T(8,128)(2,1)}), bf16[576,2048]{1,0:T(8,128)(2,1)}) %all-gather.2.cloned.1.call-update) | async-done | bytes 2359312 | tf_op jit(solution)/shard_map/all_gather | solution.py:87
  119.1 8.2 %convolution_convert_fusion = bf16[576,2048]{1,0:T(8,128)(2,1)S(1)} fusion(bf16[576,2048]{1,0:T(8,128)(2,1)} %all-gather.2.cloned.1.call-done, bf16[2048,2048]{1,0:T(8,128)(2,1)} %param.15), kind=kOutput, calls=%fused_computation.28 | convolution fusion | flops 4833017856 | bytes 13107200 | tf_op jit(solution)/shard_map/dot_general | solution.py:86
  127.3 56.4 %all_to_all.19 = bf16[4,144,2048]{2,1,0:T(8,128)(2,1)S(1)} all-to-all(bf16[4,144,2048]{2,1,0:T(8,128)(2,1)S(1)} %bitcast.57), channel_id=1, replica_groups=mesh['groups'=2,'ctx'=4,'tp'=4] {'ctx'}, dimensions={0} | all-to-all | bytes 4718592 | tf_op jit(solution)/shard_map/all_to_all | solution.py:91
  183.7 1.6 copy.25
  185.3 0.7 copy-done.6
  186.1 31.3 %reduce-scatter.2.cloned.1.call-done = bf16[144,2048]{1,0:T(8,128)(2,1)} async-done(((bf16[144,8192]{1,0:T(8,128)(2,1)}), bf16[144,2048]{1,0:T(8,128)(2,1)}) %reduce-scatter.2.cloned.1.call-update) | async-done | bytes 589840 | tf_op jit(solution)/shard_map/reduce_scatter | solution.py:94
  217.4 1.2 add_convert_fusion
  218.6 0.3 convolution_bitcast_fusion
  219.0 32.1 %all-reduce.3 = (f32[16]{0:T(128)S(1)}, f32[16]{0:T(128)S(1)}) all-reduce(f32[16]{0:T(128)S(1)} %convolution_bitcast_fusion.1, f32[16]{0:T(128)S(1)} %broadcast_select_fusion.1), channel_id=1, replica_groups=mesh['groups'=2,'ctx'=4,'tp'=4] {'ctx','tp'}, use_global_device_ids=true, to_apply=%region_5.6 | all-reduce | flops 32 | bytes 256 | tf_op jit(solution)/shard_map/psum | solution.py:102
  251.1 0.5 maximum_divide_fusion
  (123 shorter events, 4.5 us)
Async XLA Ops:
  7.2 111.9 %all-gather.2.cloned.1.call-start = ((), (), s32[]{:S(2)}) async-start(), calls=%async_computation.2 | async-start | bytes 2949120 | tf_op jit(solution)/shard_map/all_gather | solution.py:87
  21.1 1.4 copy-start.2
  22.3 14.3 %copy-start.3 = (bf16[144,256]{1,0:T(8,128)(2,1)S(1)}, bf16[144,256]{1,0:T(8,128)(2,1)}, u32[]{:S(2)}) copy-start(bf16[144,256]{1,0:T(8,128)(2,1)} %param.13) | copy-start | bytes 221188
  22.5 28.5 %copy-start.4 = (s32[144]{0:T(256)S(1)}, s32[144]{0:T(256)}, u32[]{:S(2)}) copy-start(s32[144]{0:T(256)} %param.17) | copy-start | bytes 1732
  22.5 28.5 %copy-start.5 = (s32[144]{0:T(256)S(1)}, s32[144]{0:T(256)}, u32[]{:S(2)}) copy-start(s32[144]{0:T(256)} %param.18) | copy-start | bytes 1732
  68.9 148.5 %reduce-scatter.2.cloned.1.call-start = ((), (), s32[]{:S(2)}) async-start(), calls=%async_computation.3 | async-start | bytes 2949120 | tf_op jit(solution)/shard_map/reduce_scatter | solution.py:94
  185.3 0.7 copy-start.6
  185.3 0.7 copy-start.7
  185.3 32.1 %copy-start.1 = (bf16[144,2048]{1,0:T(8,128)(2,1)S(1)}, bf16[144,2048]{1,0:T(8,128)(2,1)}, u32[]{:S(2)}) copy-start(bf16[144,2048]{1,0:T(8,128)(2,1)} %param.14) | copy-start | bytes 1769476
  218.6 33.0 %copy-start = (bf16[144,2048]{1,0:T(8,128)(2,1)}, bf16[144,2048]{1,0:T(8,128)(2,1)S(1)}, u32[]{:S(2)}) copy-start(bf16[144,2048]{1,0:T(8,128)(2,1)S(1)} %add_convert_fusion) | copy-start | bytes 1769476
Sparse Core Ops, SparseCore 0:
  69.0 50.0 all-gather.1
  185.4 31.9 reduce-scatter.1
where the time goes:
time: 259 us; the launch traced here: 258 us
  blocking collectives  127 us (49%)
  waiting for transfers between devices  81.5 us (31%)
  matrix products  19.1 us (7%)
  between operations  14.9 us (6%)
  local copies, waits for them, and re-layouts  10.1 us (4%)
  other arithmetic  5.05 us (2%)
    all_to_all x1, blocking collectives, shards(): lax.all_to_all(partial_value, 'ctx', split_axis=0, concat_axis=1, tiled=T...  56.4 us
    all_gather x1, waiting for transfers between devices, shards(): lax.all_gather(attention, 'ctx', axis=0, tiled=True)  50.1 us
    psum x1, blocking collectives, shards(): totals, counts = lax.psum((local_sum, local_count), ('ctx', 'tp'))  32.1 us
    reduce_scatter x1, waiting for transfers between devices, shards(): lax.psum_scatter(term_rows.astype(jnp.bfloat16), 'tp', scatter_dimension=...  31.3 us
    all_gather x1, blocking collectives, shards(): value_piece = lax.all_gather(values, 'ctx', axis=0, tiled=True)  14.3 us
    all_gather x1, blocking collectives, shards(): key_piece = lax.all_gather(keys, 'ctx', axis=0, tiled=True)  14 us
    unnamed x1, blocking collectives  10 us
    dot_general x1, matrix products, shards(): jnp.dot(lax.all_gather(attention, 'ctx', axis=0, tiled=True), out_weight,...  8.18 us
  transfers between devices with their start and end apart: 2, of which 2 were waited for; matrix products, arithmetic and copies ran while one was open for 0% of the time, Pallas kernels for 0%

commit v1 on v0

--- a/solution.py
+++ b/solution.py
@@ -1,8 +1,11 @@
+import functools
 import math
 
 import jax
 import jax.numpy as jnp
 from jax import lax
+from jax.experimental import pallas as pl
+from jax.experimental.pallas import tpu as pltpu
 from jax.sharding import PartitionSpec as P
 
 HEAD_SIZE = 128
@@ -104,9 +107,393 @@
     return (hidden_out, turn_means)
 
 
+MESH = pl.DeviceIdType.MESH
+F32 = jnp.float32
+BF16 = jnp.bfloat16
+
+
+def kernel(
+    dims, q_ref, k_ref, v_ref, code_ref, qcode_ref, tid_ref, vh_ref, res_hbm, w_hbm,
+    out_ref, mean_ref,
+    kg, vg, cg, ccol, qs, ot, att, wv, part, rs, red, fin, resv, tot,
+    k_send, v_send, c_send, k_recv, v_recv, c_recv, att_send, att_recv,
+    rs_send, rs_recv, fin_send, fin_recv, tot_send, tot_recv, w_sem, res_sem,
+):
+    n, tn, rows, groups, per, cb, lanes = dims
+    c = lax.axis_index("ctx")
+    t = lax.axis_index("tp")
+    keys_all = n * rows
+    half = per * HEAD_SIZE
+    scale = 1.0 / math.sqrt(HEAD_SIZE)
+
+    def w_copy(i):
+        return pltpu.make_async_copy(
+            w_hbm.at[:, pl.ds(pl.multiple_of(i * cb, 128), cb)], wv.at[i], w_sem.at[i]
+        )
+
+    res_copy = pltpu.make_async_copy(res_hbm, resv, res_sem)
+    for i in range(tn):
+        w_copy(i).start()
+    res_copy.start()
+
+    barrier = pltpu.get_barrier_semaphore()
+
+    def greet(i, _):
+        other = lax.rem(c * tn + t + 1 + i, n * tn)
+        pl.semaphore_signal(
+            barrier, inc=1, device_id={"ctx": other // tn, "tp": lax.rem(other, tn)},
+            device_id_type=MESH,
+        )
+        return 0
+
+    lax.fori_loop(0, n * tn - 1, greet, 0)
+    kg[c] = k_ref[...]
+    vg[c] = v_ref[...]
+    cg[c] = code_ref[...]
+    pl.semaphore_wait(barrier, n * tn - 1)
+
+    def kv_copies(s, d, own):
+        dev = {"ctx": c + 1 - 2 * d}
+        out = []
+        for src, buf, snd, rcv in (
+            (k_ref, kg, k_send, k_recv),
+            (v_ref, vg, v_send, v_recv),
+            (code_ref, cg, c_send, c_recv),
+        ):
+            out.append(
+                pltpu.make_async_remote_copy(
+                    src_ref=src if own else buf.at[s], dst_ref=buf.at[s],
+                    send_sem=snd.at[d, s], recv_sem=rcv.at[s],
+                    device_id=dev, device_id_type=MESH,
+                )
+            )
+        return out
+
+    def att_copy(s, g, d):
+        return pltpu.make_async_remote_copy(
+            src_ref=att.at[s, g], dst_ref=att.at[s, g],
+            send_sem=att_send.at[d, s, g], recv_sem=att_recv.at[s, g],
+            device_id={"ctx": c + 1 - 2 * d}, device_id_type=MESH,
+        )
+
+    def rs_copy(s, i):
+        return pltpu.make_async_remote_copy(
+            src_ref=part.at[s, i], dst_ref=rs.at[s, t],
+            send_sem=rs_send.at[s, i], recv_sem=rs_recv.at[s, t],
+            device_id={"tp": i}, device_id_type=MESH,
+        )
+
+    def rs_arrival(s, i):
+        return pltpu.make_async_remote_copy(
+            src_ref=part.at[s, i], dst_ref=rs.at[s, i],
+            send_sem=rs_send.at[s, i], recv_sem=rs_recv.at[s, i],
+            device_id={"tp": i}, device_id_type=MESH,
+        )
+
+    def fin_copy(s):
+        return pltpu.make_async_remote_copy(
+            src_ref=red.at[s], dst_ref=fin.at[t],
+            send_sem=fin_send.at[s], recv_sem=fin_recv.at[t],
+            device_id={"ctx": s, "tp": c}, device_id_type=MESH,
+        )
+
+    def fin_arrival(i):
+        return pltpu.make_async_remote_copy(
+            src_ref=red.at[0], dst_ref=fin.at[i],
+            send_sem=fin_send.at[0], recv_sem=fin_recv.at[i],
+            device_id={"ctx": t, "tp": i}, device_id_type=MESH,
+        )
+
+    def goes(s, d):
+        if d == 0:
+            return (s <= c) & (c < n - 1)
+        return (s >= c) & (c > 0)
+
+    for d in range(2):
+        @pl.when(goes(c, d))
+        def _():
+            for cp in kv_copies(c, d, True):
+                cp.start()
+
+    for g in range(groups):
+        for h in range(per):
+            col = (g * per + h) * HEAD_SIZE
+            qs[g, h * rows:(h + 1) * rows, :] = q_ref[:, col:col + HEAD_SIZE]
+
+    def order(m):
+        low = c
+        high = n - 1 - c
+        both = jnp.minimum(low, high)
+        near = jnp.where(lax.rem(m, 2) == 1, c - (m + 1) // 2, c + m // 2)
+        far = jnp.where(low > high, c - (m - high), c + (m - low))
+        return jnp.where(m <= 2 * both, near, far)
+
+    def kv_step(m, _):
+        s = order(m)
+        for cp in kv_copies(s, 0, False):
+            cp.wait_recv()
+        for d in range(2):
+            @pl.when(goes(s, d))
+            def _():
+                for cp in kv_copies(s, d, False):
+                    cp.start()
+        return 0
+
+    lax.fori_loop(1, n, kv_step, 0)
+
+    for s in range(n):
+        block = jnp.broadcast_to(cg[s, 0:1, :], (128, cg.shape[2]))
+        ccol[s] = block.T[:rows, 0:1]
+
+    for g in range(groups):
+        sl = slice(g * HEAD_SIZE, (g + 1) * HEAD_SIZE)
+
+        def score_step(i, _):
+            span = pl.ds(pl.multiple_of(i * lanes, 128), lanes)
+            keys = kg[:, :, sl].reshape(keys_all, HEAD_SIZE)
+            vals = vg[:, :, sl].reshape(keys_all, HEAD_SIZE)
+            s = lax.dot_general(
+                keys, qs[g, span, :], (((1,), (1,)), ((), ())), preferred_element_type=F32
+            ) * scale
+            cj = ccol[...].reshape(keys_all, 1)
+            allowed = (cj <= qcode_ref[0:1, span]) & (cj >= qcode_ref[1:2, span])
+            s = jnp.where(allowed, s, -1e30)
+            top = jnp.max(s, axis=0, keepdims=True)
+            p = jnp.where(allowed, jnp.exp(s - top), 0.0)
+            den = jnp.sum(p, axis=0, keepdims=True)
+            o = lax.dot_general(
+                vals, p.astype(BF16), (((0,), (0,)), ((), ())), preferred_element_type=F32
+            )
+            ot[span, :] = (o / den).T.astype(BF16)
+            return 0
+
+        lax.fori_loop(0, per * rows // lanes, score_step, 0)
+        for h in range(per):
+            att[c, g, :, h * HEAD_SIZE:(h + 1) * HEAD_SIZE] = ot[h * rows:(h + 1) * rows, :]
+        for d in range(2):
+            @pl.when(goes(c, d))
+            def _():
+                att_copy(c, g, d).start()
+
+    for i in range(tn):
+        w_copy(i).wait()
+
+    def reduce_send(s):
+        total = None
+        for i in range(tn):
+            @pl.when(t != i)
+            def _():
+                rs_arrival(s, i).wait_recv()
+        for i in range(tn):
+            term = rs[s, i].astype(F32)
+            total = term if total is None else total + term
+        summed = total.astype(BF16)
+        mine = (s == c) & (t == c)
+
+        @pl.when(mine)
+        def _():
+            fin[t] = summed
+
+        @pl.when(jnp.logical_not(mine))
+        def _():
+            red[s] = summed
+            fin_copy(s).start()
+
+    def step(m, _):
+        @pl.when(m < n)
+        def _():
+            s = order(m)
+
+            @pl.when(m > 0)
+            def _():
+                for g in range(groups):
+                    att_copy(s, g, 0).wait_recv()
+                    for d in range(2):
+                        @pl.when(goes(s, d))
+                        def _():
+                            att_copy(s, g, d).start()
+
+        @pl.when(m > 0)
+        def _():
+            reduce_send(order(m - 1))
+
+        @pl.when(m < n)
+        def _():
+            s = order(m)
+
+            def column(j, _):
+                i = lax.rem(t + 1 + j, tn)
+                acc = None
+                for g in range(groups):
+                    prod = jnp.dot(
+                        att[s, g], wv[i, g * half:(g + 1) * half, :],
+                        preferred_element_type=F32,
+                    )
+                    acc = prod if acc is None else acc + prod
+                value = acc.astype(BF16)
+
+                @pl.when(i == t)
+                def _():
+                    rs[s, t] = value
+
+                @pl.when(i != t)
+                def _():
+                    part[s, i] = value
+                    rs_copy(s, i).start()
+
+                return 0
+
+            lax.fori_loop(0, tn, column, 0)
+
+        return 0
+
+    lax.fori_loop(0, n + 1, step, 0)
+
+    res_copy.wait()
+    score = jnp.zeros((rows, 1), F32)
+    for i in range(tn):
+        @pl.when(jnp.logical_not((c == t) & (t == i)))
+        def _():
+            fin_arrival(i).wait_recv()
+        span = slice(i * cb, (i + 1) * cb)
+        hidden = (resv[:, span].astype(F32) + fin[i].astype(F32)).astype(BF16)
+        out_ref[:, span] = hidden
+        score = score + jnp.sum(
+            hidden.astype(F32) * vh_ref[:, span].astype(F32), axis=1, keepdims=True
+        )
+    turn = lax.broadcasted_iota(jnp.int32, (rows, 128), 1)
+    hot = (tid_ref[...] == turn).astype(F32)
+    sums = jnp.sum(hot * score, axis=0, keepdims=True)
+    counts = jnp.sum(hot, axis=0, keepdims=True)
+    counts = counts * jnp.where(t == 0, 1.0, 0.0)
+    row = lax.broadcasted_iota(jnp.int32, (8, 128), 0)
+    me = c * tn + t
+    tot[me] = jnp.where(row == 0, sums, jnp.where(row == 1, counts, 0.0))
+
+    def tot_copy(j):
+        other = lax.rem(me + j, n * tn)
+        return pltpu.make_async_remote_copy(
+            src_ref=tot.at[me], dst_ref=tot.at[me],
+            send_sem=tot_send.at[other], recv_sem=tot_recv.at[me],
+            device_id={"ctx": other // tn, "tp": lax.rem(other, tn)}, device_id_type=MESH,
+        )
+
+    def tot_arrival(j):
+        other = lax.rem(me + j, n * tn)
+        return pltpu.make_async_remote_copy(
+            src_ref=tot.at[me], dst_ref=tot.at[other],
+            send_sem=tot_send.at[other], recv_sem=tot_recv.at[other],
+            device_id={"ctx": other // tn, "tp": lax.rem(other, tn)}, device_id_type=MESH,
+        )
+
+    def tot_start(j, _):
+        tot_copy(j).start()
+        return 0
+
+    lax.fori_loop(1, n * tn, tot_start, 0)
+
+    def drain(s, _):
+        for d in range(2):
+            @pl.when(goes(s, d))
+            def _():
+                for cp in kv_copies(s, d, False):
+                    cp.wait_send()
+                for g in range(groups):
+                    att_copy(s, g, d).wait_send()
+        for i in range(tn):
+            @pl.when(t != i)
+            def _():
+                rs_copy(s, i).wait_send()
+
+        @pl.when(jnp.logical_not((s == c) & (t == c)))
+        def _():
+            fin_copy(s).wait_send()
+
+        return 0
+
+    lax.fori_loop(0, n, drain, 0)
+
+    def tot_wait(j, _):
+        tot_arrival(j).wait_recv()
+        tot_copy(j).wait_send()
+        return 0
+
+    lax.fori_loop(1, n * tn, tot_wait, 0)
+    whole = jnp.sum(tot[...], axis=0)
+    mean_ref[...] = whole[0:1, :TURNS] / jnp.maximum(whole[1:2, :TURNS], 1.0)
+
+
+def fused(
+    n, tn, queries, keys, values, residual, out_weight, value_head, segment_ids, positions, turn_ids
+):
+    rows, width = queries.shape
+    groups = keys.shape[1] // HEAD_SIZE
+    per = width // keys.shape[1]
+    cols = out_weight.shape[1]
+    cb = cols // tn
+    lanes = next(x for x in (384, 256, 128) if (per * rows) % x == 0)
+    low = segment_ids * (n * rows)
+    code = low + positions
+    padded = -(-rows // 128) * 128
+    code_block = jnp.broadcast_to(jnp.pad(code, (0, padded - rows))[None, :], (8, padded))
+    qcode = jnp.stack([jnp.tile(code, per), jnp.tile(low, per)])
+    dims = (n, tn, rows, groups, per, cb, lanes)
+    vmem = pl.BlockSpec(memory_space=pltpu.VMEM)
+    hbm = pl.BlockSpec(memory_space=pl.ANY)
+    dma = pltpu.SemaphoreType.DMA
+    out, means = pl.pallas_call(
+        functools.partial(kernel, dims),
+        out_shape=(
+            jax.ShapeDtypeStruct((rows, cols), BF16),
+            jax.ShapeDtypeStruct((1, TURNS), F32),
+        ),
+        in_specs=[vmem] * 7 + [hbm] * 2,
+        out_specs=(vmem, vmem),
+        scratch_shapes=[
+            pltpu.VMEM((n, rows, groups * HEAD_SIZE), BF16),
+            pltpu.VMEM((n, rows, groups * HEAD_SIZE), BF16),
+            pltpu.VMEM((n, 8, padded), jnp.int32),
+            pltpu.VMEM((n, rows, 1), jnp.int32),
+            pltpu.VMEM((groups, per * rows, HEAD_SIZE), BF16),
+            pltpu.VMEM((per * rows, HEAD_SIZE), BF16),
+            pltpu.VMEM((n, groups, rows, per * HEAD_SIZE), BF16),
+            pltpu.VMEM((tn, width, cb), BF16),
+            pltpu.VMEM((n, tn, rows, cb), BF16),
+            pltpu.VMEM((n, tn, rows, cb), BF16),
+            pltpu.VMEM((n, rows, cb), BF16),
+            pltpu.VMEM((tn, rows, cb), BF16),
+            pltpu.VMEM((rows, cols), BF16),
+            pltpu.VMEM((n * tn, 8, 128), F32),
+            dma((2, n)), dma((2, n)), dma((2, n)),
+            dma((n,)), dma((n,)), dma((n,)),
+            dma((2, n, groups)), dma((n, groups)),
+            dma((n, tn)), dma((n, tn)),
+            dma((n,)), dma((tn,)),
+            dma((n * tn,)), dma((n * tn,)),
+            dma((tn,)), dma(()),
+        ],
+        compiler_params=pltpu.CompilerParams(
+            collective_id=0, has_side_effects=True, vmem_limit_bytes=56 * 1024 * 1024
+        ),
+    )(
+        queries, keys, values, code_block, qcode, turn_ids.reshape(rows, 1),
+        value_head.reshape(1, -1), residual, out_weight,
+    )
+    return out, means.reshape(TURNS)
+
+
+def body(n, tn, *args):
+    queries, weight = args[0], args[4]
+    rows = queries.shape[0]
+    fits = n == tn and rows % 16 == 0 and weight.shape[1] % (128 * tn) == 0
+    if fits:
+        return fused(n, tn, *args)
+    return shards(*args)
+
+
 def solution(mesh):
     return jax.shard_map(
-        shards,
+        functools.partial(body, mesh.shape["ctx"], mesh.shape["tp"]),
         mesh=mesh,
         in_specs=(
             P(("groups", "ctx"), "tp"),

time: 259 us -> 99.1 us (0.38)
  blocking collectives: 127 us -> 0 us
  Pallas kernels: 0 us -> 90.4 us
  waiting for transfers between devices: 81.5 us -> 0 us
  matrix products: 19.1 us -> 0 us
  between operations: 14.9 us -> 0.65 us
  other arithmetic: 5.05 us -> 1.3 us
  local copies, waits for them, and re-layouts: 10.1 us -> 6.57 us
    pallas_call x0 -> x1, Pallas kernels: none -> 90.4 us  [fused(): pl.pallas_call(functools.partial(kernel, dims), out_shape=(jax.ShapeDtype...]
    all_to_all x1 -> x0, blocking collectives: 56.4 us -> none  [shards(): lax.all_to_all(partial_value, 'ctx', split_axis=0, concat_axis=1, tiled=T...]
    all_gather x1 -> x0, waiting for transfers between devices: 50.1 us -> none  [shards(): lax.all_gather(attention, 'ctx', axis=0, tiled=True)]
    psum x1 -> x0, blocking collectives: 32.1 us -> none  [shards(): totals, counts = lax.psum((local_sum, local_count), ('ctx', 'tp'))]
    reduce_scatter x1 -> x0, waiting for transfers between devices: 31.3 us -> none  [shards(): lax.psum_scatter(term_rows.astype(jnp.bfloat16), 'tp', scatter_dimension=...]
    all_gather x2 -> x0, blocking collectives: 28.3 us -> none  [the longest x1 14.3 us: shards(): value_piece = lax.all_gather(values, 'ctx', axis=0, tiled=True)]
    dot_general x21 -> x0, matrix products: 19.1 us -> none  [the longest x1 8.18 us: shards(): jnp.dot(lax.all_gather(attention, 'ctx', axis=0, tiled=True), out_weight,...]
    unnamed x1 -> x0, blocking collectives: 10 us -> none
  transfers between devices with their start and end apart: 2 -> 0, of which waited for: 2 -> 0; matrix products, arithmetic and copies ran while one was open for 0% -> 0% of each run, Pallas kernels for 0% -> 0%
where the time goes in v1:
time: 99.1 us; the launch traced here: 98.9 us
  Pallas kernels  90.4 us (91%)
  local copies, waits for them, and re-layouts  6.57 us (7%)
  other arithmetic  1.3 us (1%)
    pallas_call x1, Pallas kernels, fused(): pl.pallas_call(functools.partial(kernel, dims), out_shape=(jax.ShapeDtype...  90.4 us
    unnamed x2, local copies, waits for them, and re-layouts  3.1 us

profile of v1, /device:TPU:0, one launch (start us, length us, event | category | flops | bytes accessed | tf_op | source)
XLA Modules:
  0.0 98.9 jit_solution(10379632525157793282)
XLA Ops:
  0.6 0.7 broadcast_multiply_fusion
  1.3 0.1 stack_tile.6
  1.4 0.6 broadcast_in_dim.2.code_ref
  2.0 0.1 stack_tile.7
  2.1 0.6 pad_add_fusion.qcode_ref
  2.7 1.3 %reshape.17.vh_ref = bf16[1,2048]{1,0:T(2,128)(2,1)} reshape(bf16[2048]{0:T(1024)(128)(2,1)} %param.14) | data formatting | bytes 8192 | tf_op jit(solution)/shard_map/reshape | solution.py:480
  4.0 1.4 %copy.11.tid_ref = s32[144,1]{1,0:T(8,128)} copy(s32[144,1]{0,1:T(1,128)} %bitcast.2) | data formatting | bytes 1152 | tf_op jit(solution)/shard_map/reshape | solution.py:479
  5.4 90.4 %shard_map.104 = (bf16[144,2048]{1,0:T(8,128)(2,1)}, f32[1,16]{1,0:T(1,128)}) custom-call(bf16[144,2048]{1,0:T(8,128)(2,1)} %q_ref.1, bf16[144,256]{1,0:T(8,128)(2,1)} %k_ref.1, bf16[144,256]{1,0:T(8,128)(2,1)} %v_ref.1, s32[8,256]{1,0:T(8,128)} %broadcast_in_dim.2.code_ref, s32[2,1152]{1,0:T(2,128)} %pad_add_fusion.qcode_ref, s32[144,1]{1,0:T(8,128)} %copy.11.tid_ref, ...), custom_call_target="tpu_custom_call" | custom-call | tf_op jit(solution)/shard_map/pallas_call | solution.py:444
  95.8 1.9 %copy.14 = bf16[144,2048]{1,0:T(8,128)(2,1)} copy(bf16[144,2048]{1,0:T(8,128)(2,1)} %get-tuple-element.10) | data formatting | bytes 1179648
  97.7 1.2 %copy.15 = f32[16]{0:T(128)} copy(f32[16]{0:T(128)} %bitcast.3) | data formatting | bytes 128
  (3 shorter events, 0.0 us)

commit v2 on v1

--- a/solution.py
+++ b/solution.py
@@ -113,9 +113,9 @@
 
 
 def kernel(
-    dims, q_ref, k_ref, v_ref, code_ref, qcode_ref, tid_ref, vh_ref, res_hbm, w_hbm,
+    dims, q_ref, k_ref, v_ref, seg_ref, pos_ref, tid_ref, vh_ref, res_hbm, w_hbm,
     out_ref, mean_ref,
-    kg, vg, cg, ccol, qs, ot, att, wv, part, rs, red, fin, resv, tot,
+    kg, vg, cg, ccol, ids, tcol, qrow, qs, ot, att, wv, acc, part, rs, red, fin, resv, tot,
     k_send, v_send, c_send, k_recv, v_recv, c_recv, att_send, att_recv,
     rs_send, rs_recv, fin_send, fin_recv, tot_send, tot_recv, w_sem, res_sem,
 ):
@@ -126,16 +126,6 @@
     half = per * HEAD_SIZE
     scale = 1.0 / math.sqrt(HEAD_SIZE)
 
-    def w_copy(i):
-        return pltpu.make_async_copy(
-            w_hbm.at[:, pl.ds(pl.multiple_of(i * cb, 128), cb)], wv.at[i], w_sem.at[i]
-        )
-
-    res_copy = pltpu.make_async_copy(res_hbm, resv, res_sem)
-    for i in range(tn):
-        w_copy(i).start()
-    res_copy.start()
-
     barrier = pltpu.get_barrier_semaphore()
 
     def greet(i, _):
@@ -147,27 +137,40 @@
         return 0
 
     lax.fori_loop(0, n * tn - 1, greet, 0)
-    kg[c] = k_ref[...]
-    vg[c] = v_ref[...]
-    cg[c] = code_ref[...]
+
+    def w_copy(i):
+        return pltpu.make_async_copy(
+            w_hbm.at[:, pl.ds(pl.multiple_of(i * cb, 128), cb)], wv.at[i], w_sem.at[i]
+        )
+
+    res_copy = pltpu.make_async_copy(res_hbm, resv, res_sem)
+
+    ids[...] = jnp.zeros_like(ids)
+    low = seg_ref[...].reshape(1, rows) * keys_all
+    ids[0:1, 0:rows] = low + pos_ref[...].reshape(1, rows)
+    ids[1:2, 0:rows] = low
+    ids[2:3, 0:rows] = tid_ref[...].reshape(1, rows)
+    cg[c] = ids[0:8, :]
+    for g in range(groups):
+        kg[g, c] = k_ref[:, g * HEAD_SIZE:(g + 1) * HEAD_SIZE]
+        vg[g, c] = v_ref[:, g * HEAD_SIZE:(g + 1) * HEAD_SIZE]
     pl.semaphore_wait(barrier, n * tn - 1)
 
-    def kv_copies(s, d, own):
-        dev = {"ctx": c + 1 - 2 * d}
-        out = []
-        for src, buf, snd, rcv in (
-            (k_ref, kg, k_send, k_recv),
-            (v_ref, vg, v_send, v_recv),
-            (code_ref, cg, c_send, c_recv),
-        ):
-            out.append(
-                pltpu.make_async_remote_copy(
-                    src_ref=src if own else buf.at[s], dst_ref=buf.at[s],
-                    send_sem=snd.at[d, s], recv_sem=rcv.at[s],
-                    device_id=dev, device_id_type=MESH,
-                )
+    def kv_copies(g, src, dst, slot):
+        dev = {"ctx": dst}
+        span = slice(g * HEAD_SIZE, (g + 1) * HEAD_SIZE)
+        plan = [
+            (k_ref.at[:, span], kg.at[g, src], k_send.at[g, slot], k_recv.at[g, src]),
+            (v_ref.at[:, span], vg.at[g, src], v_send.at[g, slot], v_recv.at[g, src]),
+        ]
+        if g == 0:
+            plan.insert(0, (cg.at[src], cg.at[src], c_send.at[slot], c_recv.at[src]))
+        return [
+            pltpu.make_async_remote_copy(
+                src_ref=a, dst_ref=b, send_sem=x, recv_sem=y, device_id=dev, device_id_type=MESH
             )
-        return out
+            for a, b, x, y in plan
+        ]
 
     def att_copy(s, g, d):
         return pltpu.make_async_remote_copy(
@@ -209,54 +212,44 @@
             return (s <= c) & (c < n - 1)
         return (s >= c) & (c > 0)
 
-    for d in range(2):
-        @pl.when(goes(c, d))
-        def _():
-            for cp in kv_copies(c, d, True):
+    for g in range(groups):
+        for j in range(1, n):
+            dst = lax.rem(c + j, n)
+            for cp in kv_copies(g, c, dst, dst):
                 cp.start()
+    for i in range(tn):
+        w_copy(i).start()
+    res_copy.start()
 
     for g in range(groups):
         for h in range(per):
             col = (g * per + h) * HEAD_SIZE
             qs[g, h * rows:(h + 1) * rows, :] = q_ref[:, col:col + HEAD_SIZE]
-
-    def order(m):
-        low = c
-        high = n - 1 - c
-        both = jnp.minimum(low, high)
-        near = jnp.where(lax.rem(m, 2) == 1, c - (m + 1) // 2, c + m // 2)
-        far = jnp.where(low > high, c - (m - high), c + (m - low))
-        return jnp.where(m <= 2 * both, near, far)
-
-    def kv_step(m, _):
-        s = order(m)
-        for cp in kv_copies(s, 0, False):
-            cp.wait_recv()
-        for d in range(2):
-            @pl.when(goes(s, d))
-            def _():
-                for cp in kv_copies(s, d, False):
-                    cp.start()
-        return 0
-
-    lax.fori_loop(1, n, kv_step, 0)
-
-    for s in range(n):
-        block = jnp.broadcast_to(cg[s, 0:1, :], (128, cg.shape[2]))
-        ccol[s] = block.T[:rows, 0:1]
+    idcol = ids[...].T[:rows, :]
+    tcol[...] = idcol[:, 2:3]
+    qrow[...] = jnp.concatenate([idcol] * per, axis=0).T[0:8, :]
 
     for g in range(groups):
-        sl = slice(g * HEAD_SIZE, (g + 1) * HEAD_SIZE)
+        for j in range(1, n):
+            src = lax.rem(c + n - j, n)
+            for cp in kv_copies(g, src, src, src):
+                cp.wait_recv()
+        if g == 0:
+            for s in range(n):
+                ids[s:s + 1, :] = cg[s, 0:1, :]
+            columns = ids[...].T[:rows, :]
+            for s in range(n):
+                ccol[s] = columns[:, s:s + 1]
 
         def score_step(i, _):
             span = pl.ds(pl.multiple_of(i * lanes, 128), lanes)
-            keys = kg[:, :, sl].reshape(keys_all, HEAD_SIZE)
-            vals = vg[:, :, sl].reshape(keys_all, HEAD_SIZE)
+            keys = kg[g].reshape(keys_all, HEAD_SIZE)
+            vals = vg[g].reshape(keys_all, HEAD_SIZE)
             s = lax.dot_general(
                 keys, qs[g, span, :], (((1,), (1,)), ((), ())), preferred_element_type=F32
             ) * scale
             cj = ccol[...].reshape(keys_all, 1)
-            allowed = (cj <= qcode_ref[0:1, span]) & (cj >= qcode_ref[1:2, span])
+            allowed = (cj <= qrow[0:1, span]) & (cj >= qrow[1:2, span])
             s = jnp.where(allowed, s, -1e30)
             top = jnp.max(s, axis=0, keepdims=True)
             p = jnp.where(allowed, jnp.exp(s - top), 0.0)
@@ -278,12 +271,47 @@
     for i in range(tn):
         w_copy(i).wait()
 
+    def column_of(j):
+        if tn == 4:
+            odd = lax.rem(t, 2)
+            shift = jnp.where(
+                j == 0, 2, jnp.where(j == 1, 3 - 2 * odd, jnp.where(j == 2, 1 + 2 * odd, 0))
+            )
+            return lax.rem(t + shift, tn)
+        return lax.rem(t + 1 + j, tn)
+
+    def project(s, side, g):
+        def column(j, _):
+            i = column_of(j)
+            prod = jnp.dot(
+                att[s, g], wv[i, g * half:(g + 1) * half, :], preferred_element_type=F32
+            )
+            if g > 0:
+                prod = acc[side, i] + prod
+            if g < groups - 1:
+                acc[side, i] = prod
+                return 0
+            value = prod.astype(BF16)
+
+            @pl.when(i == t)
+            def _():
+                rs[s, t] = value
+
+            @pl.when(i != t)
+            def _():
+                part[s, i] = value
+                rs_copy(s, i).start()
+
+            return 0
+
+        lax.fori_loop(0, tn, column, 0)
+
     def reduce_send(s):
-        total = None
         for i in range(tn):
             @pl.when(t != i)
             def _():
                 rs_arrival(s, i).wait_recv()
+        total = None
         for i in range(tn):
             term = rs[s, i].astype(F32)
             total = term if total is None else total + term
@@ -299,55 +327,38 @@
             red[s] = summed
             fin_copy(s).start()
 
-    def step(m, _):
-        @pl.when(m < n)
-        def _():
-            s = order(m)
-
-            @pl.when(m > 0)
-            def _():
-                for g in range(groups):
-                    att_copy(s, g, 0).wait_recv()
-                    for d in range(2):
-                        @pl.when(goes(s, d))
-                        def _():
-                            att_copy(s, g, d).start()
-
-        @pl.when(m > 0)
-        def _():
-            reduce_send(order(m - 1))
-
-        @pl.when(m < n)
-        def _():
-            s = order(m)
-
-            def column(j, _):
-                i = lax.rem(t + 1 + j, tn)
-                acc = None
-                for g in range(groups):
-                    prod = jnp.dot(
-                        att[s, g], wv[i, g * half:(g + 1) * half, :],
-                        preferred_element_type=F32,
-                    )
-                    acc = prod if acc is None else acc + prod
-                value = acc.astype(BF16)
-
-                @pl.when(i == t)
-                def _():
-                    rs[s, t] = value
-
-                @pl.when(i != t)
-                def _():
-                    part[s, i] = value
-                    rs_copy(s, i).start()
-
-                return 0
-
-            lax.fori_loop(0, tn, column, 0)
-
+    def both_sides(k, act):
+        def one(side, _):
+            s = c + k * (2 * side - 1)
+
+            @pl.when((s >= 0) & (s < n) & ((k > 0) | (side == 0)))
+            def _():
+                act(s, side)
+
+            return 0
+
+        lax.fori_loop(0, 2, one, 0)
+
+    for g in range(groups):
+        project(c, 0, g)
+
+    def step(k, _):
+        for g in range(groups):
+            def take(s, side):
+                att_copy(s, g, 0).wait_recv()
+                for d in range(2):
+                    @pl.when(goes(s, d))
+                    def _():
+                        att_copy(s, g, d).start()
+
+            both_sides(k, take)
+            both_sides(k, lambda s, side: project(s, side, g))
+            if g == 0:
+                both_sides(k - 1, lambda s, side: reduce_send(s))
         return 0
 
-    lax.fori_loop(0, n + 1, step, 0)
+    lax.fori_loop(1, n, step, 0)
+    both_sides(n - 1, lambda s, side: reduce_send(s))
 
     res_copy.wait()
     score = jnp.zeros((rows, 1), F32)
@@ -359,10 +370,10 @@
         hidden = (resv[:, span].astype(F32) + fin[i].astype(F32)).astype(BF16)
         out_ref[:, span] = hidden
         score = score + jnp.sum(
-            hidden.astype(F32) * vh_ref[:, span].astype(F32), axis=1, keepdims=True
+            hidden.astype(F32) * vh_ref[span].astype(F32).reshape(1, cb), axis=1, keepdims=True
         )
     turn = lax.broadcasted_iota(jnp.int32, (rows, 128), 1)
-    hot = (tid_ref[...] == turn).astype(F32)
+    hot = (tcol[...] == turn).astype(F32)
     sums = jnp.sum(hot * score, axis=0, keepdims=True)
     counts = jnp.sum(hot, axis=0, keepdims=True)
     counts = counts * jnp.where(t == 0, 1.0, 0.0)
@@ -393,11 +404,15 @@
     lax.fori_loop(1, n * tn, tot_start, 0)
 
     def drain(s, _):
+        @pl.when(s != c)
+        def _():
+            for g in range(groups):
+                for cp in kv_copies(g, c, s, s):
+                    cp.wait_send()
+
         for d in range(2):
             @pl.when(goes(s, d))
             def _():
-                for cp in kv_copies(s, d, False):
-                    cp.wait_send()
                 for g in range(groups):
                     att_copy(s, g, d).wait_send()
         for i in range(tn):
@@ -432,11 +447,7 @@
     cols = out_weight.shape[1]
     cb = cols // tn
     lanes = next(x for x in (384, 256, 128) if (per * rows) % x == 0)
-    low = segment_ids * (n * rows)
-    code = low + positions
     padded = -(-rows // 128) * 128
-    code_block = jnp.broadcast_to(jnp.pad(code, (0, padded - rows))[None, :], (8, padded))
-    qcode = jnp.stack([jnp.tile(code, per), jnp.tile(low, per)])
     dims = (n, tn, rows, groups, per, cb, lanes)
     vmem = pl.BlockSpec(memory_space=pltpu.VMEM)
     hbm = pl.BlockSpec(memory_space=pl.ANY)
@@ -450,22 +461,26 @@
         in_specs=[vmem] * 7 + [hbm] * 2,
         out_specs=(vmem, vmem),
         scratch_shapes=[
-            pltpu.VMEM((n, rows, groups * HEAD_SIZE), BF16),
-            pltpu.VMEM((n, rows, groups * HEAD_SIZE), BF16),
+            pltpu.VMEM((groups, n, rows, HEAD_SIZE), BF16),
+            pltpu.VMEM((groups, n, rows, HEAD_SIZE), BF16),
             pltpu.VMEM((n, 8, padded), jnp.int32),
             pltpu.VMEM((n, rows, 1), jnp.int32),
+            pltpu.VMEM((128, padded), jnp.int32),
+            pltpu.VMEM((rows, 1), jnp.int32),
+            pltpu.VMEM((8, per * rows), jnp.int32),
             pltpu.VMEM((groups, per * rows, HEAD_SIZE), BF16),
             pltpu.VMEM((per * rows, HEAD_SIZE), BF16),
             pltpu.VMEM((n, groups, rows, per * HEAD_SIZE), BF16),
             pltpu.VMEM((tn, width, cb), BF16),
+            pltpu.VMEM((2, tn, rows, cb), F32),
             pltpu.VMEM((n, tn, rows, cb), BF16),
             pltpu.VMEM((n, tn, rows, cb), BF16),
             pltpu.VMEM((n, rows, cb), BF16),
             pltpu.VMEM((tn, rows, cb), BF16),
             pltpu.VMEM((rows, cols), BF16),
             pltpu.VMEM((n * tn, 8, 128), F32),
-            dma((2, n)), dma((2, n)), dma((2, n)),
-            dma((n,)), dma((n,)), dma((n,)),
+            dma((groups, n)), dma((groups, n)), dma((n,)),
+            dma((groups, n)), dma((groups, n)), dma((n,)),
             dma((2, n, groups)), dma((n, groups)),
             dma((n, tn)), dma((n, tn)),
             dma((n,)), dma((tn,)),
@@ -476,8 +491,8 @@
             collective_id=0, has_side_effects=True, vmem_limit_bytes=56 * 1024 * 1024
         ),
     )(
-        queries, keys, values, code_block, qcode, turn_ids.reshape(rows, 1),
-        value_head.reshape(1, -1), residual, out_weight,
+        queries, keys, values, segment_ids, positions, turn_ids,
+        value_head, residual, out_weight,
     )
     return out, means.reshape(TURNS)
 
@@ -485,7 +500,7 @@
 def body(n, tn, *args):
     queries, weight = args[0], args[4]
     rows = queries.shape[0]
-    fits = n == tn and rows % 16 == 0 and weight.shape[1] % (128 * tn) == 0
+    fits = n == tn and n <= 128 and rows % 16 == 0 and weight.shape[1] % (128 * tn) == 0
     if fits:
         return fused(n, tn, *args)
     return shards(*args)

time: 99.1 us -> 91.6 us (0.924)
  local copies, waits for them, and re-layouts: 6.57 us -> 3.1 us
  Pallas kernels: 90.4 us -> 87.7 us
  other arithmetic: 1.3 us -> 0 us
    reshape x2 -> x0, local copies, waits for them, and re-layouts: 2.69 us -> none  [the longest x1 1.42 us: fused(): turn_ids.reshape(rows, 1)]
    pallas_call x1, Pallas kernels: 90.4 us -> 87.7 us  [fused(): pl.pallas_call(functools.partial(kernel, dims), out_shape=(jax.ShapeDtype...]
where the time goes in v2:
time: 91.6 us; the launch traced here: 91.4 us
  Pallas kernels  87.7 us (96%)
  local copies, waits for them, and re-layouts  3.1 us (3%)
    pallas_call x1, Pallas kernels, fused(): pl.pallas_call(functools.partial(kernel, dims), out_shape=(jax.ShapeDtype...  87.7 us
    unnamed x2, local copies, waits for them, and re-layouts  3.1 us

profile of v2, /device:TPU:0, one launch (start us, length us, event | category | flops | bytes accessed | tf_op | source)
XLA Modules:
  0.0 91.4 jit_solution(17989439108280710466)
XLA Ops:
  0.6 87.7 %shard_map.104 = (bf16[144,2048]{1,0:T(8,128)(2,1)}, f32[1,16]{1,0:T(1,128)}) custom-call(bf16[144,2048]{1,0:T(8,128)(2,1)} %q_ref.1, bf16[144,256]{1,0:T(8,128)(2,1)} %k_ref.1, bf16[144,256]{1,0:T(8,128)(2,1)} %v_ref.1, s32[144]{0:T(256)} %seg_ref.1, s32[144]{0:T(256)} %pos_ref.1, s32[144]{0:T(256)} %tid_ref.1, bf16[2048]{0:T(1024)(128)(2,1)} %vh_ref.1, ...), custom_call_target="tpu_custom_call" | custom-call | tf_op jit(solution)/shard_map/pallas_call | solution.py:455
  88.3 1.9 %copy.13 = bf16[144,2048]{1,0:T(8,128)(2,1)} copy(bf16[144,2048]{1,0:T(8,128)(2,1)} %get-tuple-element.8) | data formatting | bytes 1179648
  90.3 1.2 %copy.14 = f32[16]{0:T(128)} copy(f32[16]{0:T(128)} %bitcast.1) | data formatting | bytes 128

commit v3 on v2

--- a/solution.py
+++ b/solution.py
@@ -119,7 +119,8 @@
     k_send, v_send, c_send, k_recv, v_recv, c_recv, att_send, att_recv,
     rs_send, rs_recv, fin_send, fin_recv, tot_send, tot_recv, w_sem, res_sem,
 ):
-    n, tn, rows, groups, per, cb, lanes = dims
+    n, tn, rows, groups, per, cb, lanes, pieces = dims
+    piece = rows // pieces
     c = lax.axis_index("ctx")
     t = lax.axis_index("tp")
     keys_all = n * rows
@@ -179,31 +180,34 @@
             device_id={"ctx": c + 1 - 2 * d}, device_id_type=MESH,
         )
 
-    def rs_copy(s, i):
-        return pltpu.make_async_remote_copy(
-            src_ref=part.at[s, i], dst_ref=rs.at[s, t],
-            send_sem=rs_send.at[s, i], recv_sem=rs_recv.at[s, t],
+    def band(p):
+        return pl.ds(p * piece, piece)
+
+    def rs_copy(s, i, p):
+        return pltpu.make_async_remote_copy(
+            src_ref=part.at[s, i, band(p)], dst_ref=rs.at[s, t, band(p)],
+            send_sem=rs_send.at[s, i, p], recv_sem=rs_recv.at[s, t, p],
             device_id={"tp": i}, device_id_type=MESH,
         )
 
-    def rs_arrival(s, i):
-        return pltpu.make_async_remote_copy(
-            src_ref=part.at[s, i], dst_ref=rs.at[s, i],
-            send_sem=rs_send.at[s, i], recv_sem=rs_recv.at[s, i],
+    def rs_arrival(s, i, p):
+        return pltpu.make_async_remote_copy(
+            src_ref=part.at[s, i, band(p)], dst_ref=rs.at[s, i, band(p)],
+            send_sem=rs_send.at[s, i, p], recv_sem=rs_recv.at[s, i, p],
             device_id={"tp": i}, device_id_type=MESH,
         )
 
-    def fin_copy(s):
-        return pltpu.make_async_remote_copy(
-            src_ref=red.at[s], dst_ref=fin.at[t],
-            send_sem=fin_send.at[s], recv_sem=fin_recv.at[t],
+    def fin_copy(s, p):
+        return pltpu.make_async_remote_copy(
+            src_ref=red.at[s, band(p)], dst_ref=fin.at[t, band(p)],
+            send_sem=fin_send.at[s, p], recv_sem=fin_recv.at[t, p],
             device_id={"ctx": s, "tp": c}, device_id_type=MESH,
         )
 
-    def fin_arrival(i):
-        return pltpu.make_async_remote_copy(
-            src_ref=red.at[0], dst_ref=fin.at[i],
-            send_sem=fin_send.at[0], recv_sem=fin_recv.at[i],
+    def fin_arrival(i, p):
+        return pltpu.make_async_remote_copy(
+            src_ref=red.at[0, band(p)], dst_ref=fin.at[i, band(p)],
+            send_sem=fin_send.at[0, p], recv_sem=fin_recv.at[i, p],
             device_id={"ctx": t, "tp": i}, device_id_type=MESH,
         )
 
@@ -300,32 +304,50 @@
             @pl.when(i != t)
             def _():
                 part[s, i] = value
-                rs_copy(s, i).start()
+
+            if tn == 4:
+                @pl.when(j == 1)
+                def _():
+                    for p in range(pieces):
+                        rs_copy(s, column_of(0), p).start()
+                        rs_copy(s, i, p).start()
+
+                @pl.when(j == 2)
+                def _():
+                    for p in range(pieces):
+                        rs_copy(s, i, p).start()
+            else:
+                @pl.when(i != t)
+                def _():
+                    for p in range(pieces):
+                        rs_copy(s, i, p).start()
 
             return 0
 
         lax.fori_loop(0, tn, column, 0)
 
     def reduce_send(s):
-        for i in range(tn):
-            @pl.when(t != i)
-            def _():
-                rs_arrival(s, i).wait_recv()
-        total = None
-        for i in range(tn):
-            term = rs[s, i].astype(F32)
-            total = term if total is None else total + term
-        summed = total.astype(BF16)
         mine = (s == c) & (t == c)
-
-        @pl.when(mine)
-        def _():
-            fin[t] = summed
-
-        @pl.when(jnp.logical_not(mine))
-        def _():
-            red[s] = summed
-            fin_copy(s).start()
+        for p in range(pieces):
+            for i in range(tn):
+                @pl.when(t != i)
+                def _():
+                    rs_arrival(s, i, p).wait_recv()
+            rng = slice(p * piece, (p + 1) * piece)
+            total = None
+            for i in range(tn):
+                term = rs[s, i, rng, :].astype(F32)
+                total = term if total is None else total + term
+            summed = total.astype(BF16)
+
+            @pl.when(mine)
+            def _():
+                fin[t, rng, :] = summed
+
+            @pl.when(jnp.logical_not(mine))
+            def _():
+                red[s, rng, :] = summed
+                fin_copy(s, p).start()
 
     def both_sides(k, act):
         def one(side, _):
@@ -361,25 +383,27 @@
     both_sides(n - 1, lambda s, side: reduce_send(s))
 
     res_copy.wait()
-    score = jnp.zeros((rows, 1), F32)
-    for i in range(tn):
-        @pl.when(jnp.logical_not((c == t) & (t == i)))
-        def _():
-            fin_arrival(i).wait_recv()
-        span = slice(i * cb, (i + 1) * cb)
-        hidden = (resv[:, span].astype(F32) + fin[i].astype(F32)).astype(BF16)
-        out_ref[:, span] = hidden
-        score = score + jnp.sum(
-            hidden.astype(F32) * vh_ref[span].astype(F32).reshape(1, cb), axis=1, keepdims=True
-        )
-    turn = lax.broadcasted_iota(jnp.int32, (rows, 128), 1)
-    hot = (tcol[...] == turn).astype(F32)
-    sums = jnp.sum(hot * score, axis=0, keepdims=True)
-    counts = jnp.sum(hot, axis=0, keepdims=True)
-    counts = counts * jnp.where(t == 0, 1.0, 0.0)
-    row = lax.broadcasted_iota(jnp.int32, (8, 128), 0)
+    line = jnp.zeros((1, 128), F32)
+    lane = lax.broadcasted_iota(jnp.int32, (piece, 128), 1)
+    one = jnp.where(t == 0, 1.0, 0.0)
+    for p in range(pieces):
+        rng = slice(p * piece, (p + 1) * piece)
+        score = jnp.zeros((piece, 1), F32)
+        for i in range(tn):
+            @pl.when(jnp.logical_not((c == t) & (t == i)))
+            def _():
+                fin_arrival(i, p).wait_recv()
+            span = slice(i * cb, (i + 1) * cb)
+            hidden = (resv[rng, span].astype(F32) + fin[i, rng, :].astype(F32)).astype(BF16)
+            out_ref[rng, span] = hidden
+            score = score + jnp.sum(
+                hidden.astype(F32) * vh_ref[span].astype(F32).reshape(1, cb), axis=1, keepdims=True
+            )
+        turn = tcol[rng, :]
+        terms = jnp.where(turn == lane, score, jnp.where(turn + 64 == lane, one, 0.0))
+        line = line + jnp.sum(terms, axis=0, keepdims=True)
     me = c * tn + t
-    tot[me] = jnp.where(row == 0, sums, jnp.where(row == 1, counts, 0.0))
+    tot[me] = line
 
     def tot_copy(j):
         other = lax.rem(me + j, n * tn)
@@ -418,11 +442,13 @@
         for i in range(tn):
             @pl.when(t != i)
             def _():
-                rs_copy(s, i).wait_send()
+                for p in range(pieces):
+                    rs_copy(s, i, p).wait_send()
 
         @pl.when(jnp.logical_not((s == c) & (t == c)))
         def _():
-            fin_copy(s).wait_send()
+            for p in range(pieces):
+                fin_copy(s, p).wait_send()
 
         return 0
 
@@ -434,8 +460,7 @@
         return 0
 
     lax.fori_loop(1, n * tn, tot_wait, 0)
-    whole = jnp.sum(tot[...], axis=0)
-    mean_ref[...] = whole[0:1, :TURNS] / jnp.maximum(whole[1:2, :TURNS], 1.0)
+    mean_ref[...] = jnp.sum(tot[...], axis=0)
 
 
 def fused(
@@ -448,7 +473,8 @@
     cb = cols // tn
     lanes = next(x for x in (384, 256, 128) if (per * rows) % x == 0)
     padded = -(-rows // 128) * 128
-    dims = (n, tn, rows, groups, per, cb, lanes)
+    pieces = 3 if rows % 48 == 0 else 1
+    dims = (n, tn, rows, groups, per, cb, lanes, pieces)
     vmem = pl.BlockSpec(memory_space=pltpu.VMEM)
     hbm = pl.BlockSpec(memory_space=pl.ANY)
     dma = pltpu.SemaphoreType.DMA
@@ -456,7 +482,7 @@
         functools.partial(kernel, dims),
         out_shape=(
             jax.ShapeDtypeStruct((rows, cols), BF16),
-            jax.ShapeDtypeStruct((1, TURNS), F32),
+            jax.ShapeDtypeStruct((1, 128), F32),
         ),
         in_specs=[vmem] * 7 + [hbm] * 2,
         out_specs=(vmem, vmem),
@@ -478,12 +504,12 @@
             pltpu.VMEM((n, rows, cb), BF16),
             pltpu.VMEM((tn, rows, cb), BF16),
             pltpu.VMEM((rows, cols), BF16),
-            pltpu.VMEM((n * tn, 8, 128), F32),
+            pltpu.VMEM((n * tn, 1, 128), F32),
             dma((groups, n)), dma((groups, n)), dma((n,)),
             dma((groups, n)), dma((groups, n)), dma((n,)),
             dma((2, n, groups)), dma((n, groups)),
-            dma((n, tn)), dma((n, tn)),
-            dma((n,)), dma((tn,)),
+            dma((n, tn, pieces)), dma((n, tn, pieces)),
+            dma((n, pieces)), dma((tn, pieces)),
             dma((n * tn,)), dma((n * tn,)),
             dma((tn,)), dma(()),
         ],
@@ -494,7 +520,7 @@
         queries, keys, values, segment_ids, positions, turn_ids,
         value_head, residual, out_weight,
     )
-    return out, means.reshape(TURNS)
+    return out, means[0, :TURNS] / jnp.maximum(means[0, 64:64 + TURNS], 1.0)
 
 
 def body(n, tn, *args):

time: 91.6 us -> 90.8 us (level)
  other arithmetic: 0 us -> 1.33 us
  local copies, waits for them, and re-layouts: 3.1 us -> 1.93 us
  Pallas kernels: 87.7 us -> 86.7 us
    div x0 -> x1, other arithmetic: none -> 1.33 us  [fused(): return (out, means[0, :TURNS] / jnp.maximum(means[0, 64:64 + TURNS], 1.0))]
    unnamed x2 -> x1, local copies, waits for them, and re-layouts: 3.1 us -> 1.93 us
    pallas_call x1, Pallas kernels: 87.7 us -> 86.7 us  [fused(): pl.pallas_call(functools.partial(kernel, dims), out_shape=(jax.ShapeDtype...]
where the time goes in v3:
time: 90.8 us; the launch traced here: 90.6 us
  Pallas kernels  86.7 us (95%)
  local copies, waits for them, and re-layouts  1.93 us (2%)
  other arithmetic  1.33 us (1%)
    pallas_call x1, Pallas kernels, fused(): pl.pallas_call(functools.partial(kernel, dims), out_shape=(jax.ShapeDtype...  86.7 us
    unnamed x1, local copies, waits for them, and re-layouts  1.93 us

profile of v3, /device:TPU:0, one launch (start us, length us, event | category | flops | bytes accessed | tf_op | source)
XLA Modules:
  0.0 90.6 jit_solution(13207972887070434706)
XLA Ops:
  0.6 86.7 %shard_map.104 = (bf16[144,2048]{1,0:T(8,128)(2,1)}, f32[1,128]{1,0:T(1,128)}) custom-call(bf16[144,2048]{1,0:T(8,128)(2,1)} %q_ref.1, bf16[144,256]{1,0:T(8,128)(2,1)} %k_ref.1, bf16[144,256]{1,0:T(8,128)(2,1)} %v_ref.1, s32[144]{0:T(256)} %seg_ref.1, s32[144]{0:T(256)} %pos_ref.1, s32[144]{0:T(256)} %tid_ref.1, bf16[2048]{0:T(1024)(128)(2,1)} %vh_ref.1, ...), custom_call_target="tpu_custom_call" | custom-call | tf_op jit(solution)/shard_map/pallas_call | solution.py:481
  87.3 1.3 %fusion = f32[16]{0:T(128)} fusion(f32[1,128]{1,0:T(1,128)} %get-tuple-element.5), kind=kLoop, calls=%fused_computation.1 | loop fusion | flops 32 | bytes 192 | tf_op jit(solution)/shard_map/div | solution.py:523
  88.6 1.9 %copy.12 = bf16[144,2048]{1,0:T(8,128)(2,1)} copy(bf16[144,2048]{1,0:T(8,128)(2,1)} %get-tuple-element.8) | data formatting | bytes 1179648

commit v4 on v3

--- a/solution.py
+++ b/solution.py
@@ -218,7 +218,7 @@
 
     for g in range(groups):
         for j in range(1, n):
-            dst = lax.rem(c + j, n)
+            dst = lax.rem(c + n - j, n)
             for cp in kv_copies(g, c, dst, dst):
                 cp.start()
     for i in range(tn):

time: 90.8 us -> 89.2 us (0.982)
  Pallas kernels: 86.7 us -> 85.1 us
    pallas_call x1, Pallas kernels: 86.7 us -> 85.1 us  [fused(): pl.pallas_call(functools.partial(kernel, dims), out_shape=(jax.ShapeDtype...]
where the time goes in v4:
time: 89.2 us; the launch traced here: 89 us
  Pallas kernels  85.1 us (95%)
  local copies, waits for them, and re-layouts  1.93 us (2%)
  other arithmetic  1.33 us (1%)
    pallas_call x1, Pallas kernels, fused(): pl.pallas_call(functools.partial(kernel, dims), out_shape=(jax.ShapeDtype...  85.1 us
    unnamed x1, local copies, waits for them, and re-layouts  1.93 us

profile of v4, /device:TPU:0, one launch (start us, length us, event | category | flops | bytes accessed | tf_op | source)
XLA Modules:
  0.0 89.0 jit_solution(12545800744468220621)
XLA Ops:
  0.6 85.1 %shard_map.104 = (bf16[144,2048]{1,0:T(8,128)(2,1)}, f32[1,128]{1,0:T(1,128)}) custom-call(bf16[144,2048]{1,0:T(8,128)(2,1)} %q_ref.1, bf16[144,256]{1,0:T(8,128)(2,1)} %k_ref.1, bf16[144,256]{1,0:T(8,128)(2,1)} %v_ref.1, s32[144]{0:T(256)} %seg_ref.1, s32[144]{0:T(256)} %pos_ref.1, s32[144]{0:T(256)} %tid_ref.1, bf16[2048]{0:T(1024)(128)(2,1)} %vh_ref.1, ...), custom_call_target="tpu_custom_call" | custom-call | tf_op jit(solution)/shard_map/pallas_call | solution.py:481
  85.7 1.3 %fusion = f32[16]{0:T(128)} fusion(f32[1,128]{1,0:T(1,128)} %get-tuple-element.5), kind=kLoop, calls=%fused_computation.1 | loop fusion | flops 32 | bytes 192 | tf_op jit(solution)/shard_map/div | solution.py:523
  87.0 1.9 %copy.12 = bf16[144,2048]{1,0:T(8,128)(2,1)} copy(bf16[144,2048]{1,0:T(8,128)(2,1)} %get-tuple-element.8) | data formatting | bytes 1179648
